TPU v7x, 32 devices: a whole 2x2x4 slice. The times are simulated.
32 devices in a mesh: seq: 2 (over x), tensor: 4 (over z), server: 4 (over y, core).
Axes of the slice: x: 2, y: 2, z: 4, core: 2. Of those that a mesh axis runs over, the one named last changes fastest.
Arguments:
- queries: bfloat16 [2048, 4096], P(('seq', 'server'), 'tensor'), may hold values from -135 to 135
- keys: bfloat16 [2048, 1024], P(('seq', 'server'), 'tensor'), may hold values from -5 to 5
- values: bfloat16 [2048, 1024], P(('seq', 'server'), 'tensor'), may hold values from -6 to 6
- doc_lengths: int32 [4], replicated, may hold values from 1 to 1024, 2048 in all
- w_out: bfloat16 [4096, 4096], P('tensor'), may hold values from -0.09375 to 0.09375
- d_out: bfloat16 [2048, 4096], P(('seq', 'server')), may hold values from -6 to 6
Outputs:
- attn_out: bfloat16 [2048, 4096], P(('seq', 'server'), 'tensor')
- grad_q: bfloat16 [2048, 4096], P(('seq', 'server'), 'tensor')
- grad_k: bfloat16 [2048, 1024], P(('seq', 'server'), 'tensor')
- grad_v: bfloat16 [2048, 1024], P(('seq', 'server'), 'tensor')
Inputs may be any that keep to these rules, and one draw needn't show every extreme that they name: `doc_lengths`: the lengths sum to 2048.
All inputs are finite; a program needn't handle non-finite values.
Results may differ from a plain program's by a relative error of at most 0.025.
Values may be sent and summed in bfloat16 or wider, within the bound.
A program may use at most 128 MiB of HBM per device.

v0:
```python
import jax
import jax.numpy as jnp
from jax import lax
from jax.sharding import PartitionSpec as P

HEAD_SIZE = 128
QUERY_BLOCK_SIZE = 128
REACH = 4


def shifted(block, axis, distance):
    devices = range(lax.axis_size(axis))
    route = [(i - distance, i) for i in devices if i - distance in devices]
    return lax.ppermute(block, axis, route)


def segment_ids(positions, doc_ends):
    return jnp.sum((doc_ends[None, :] <= positions[:, None]).astype(jnp.int32), axis=1)


def masked_scores(query_block, k_part, q_pos, k_pos, doc_ends, scale_factor):
    scores = (
        jnp.einsum("tgrd,kgd->grtk", query_block, k_part, preferred_element_type=jnp.float32)
        * scale_factor
    )
    allowed = (
        (k_pos[None, :] >= 0)
        & (k_pos[None, :] <= q_pos[:, None])
        & (segment_ids(k_pos, doc_ends)[None, :] == segment_ids(q_pos, doc_ends)[:, None])
    )
    return (allowed, scores)


def block_window(
    query_block,
    key_window,
    value_window,
    output_gradient_block,
    q_pos,
    k_pos,
    doc_ends,
    scale_factor,
):
    allowed, scores = masked_scores(query_block, key_window, q_pos, k_pos, doc_ends, scale_factor)
    masked = jnp.where(allowed, scores, -jnp.inf)
    row_top = jnp.max(masked, axis=-1, keepdims=True)
    weights = jnp.exp(masked - row_top)
    shares = weights / jnp.sum(weights, axis=-1, keepdims=True)
    lower_shares = shares.astype(jnp.bfloat16)
    output = jnp.einsum(
        "grtk,kgd->tgrd", lower_shares, value_window, preferred_element_type=jnp.float32
    ).astype(jnp.bfloat16)
    row_delta = jnp.transpose(
        jnp.sum(output.astype(jnp.float32) * output_gradient_block.astype(jnp.float32), axis=-1),
        (1, 2, 0),
    )[..., None]
    d_shares = jnp.einsum(
        "tgrd,kgd->grtk", output_gradient_block, value_window, preferred_element_type=jnp.float32
    )
    score_gradient = (shares * (d_shares - row_delta)).astype(jnp.bfloat16)
    grad_q = (
        jnp.einsum("grtk,kgd->tgrd", score_gradient, key_window, preferred_element_type=jnp.float32)
        * scale_factor
    )
    grad_k = (
        jnp.einsum(
            "acul,uacz->laz", score_gradient, query_block, preferred_element_type=jnp.float32
        )
        * scale_factor
    )
    grad_v = jnp.einsum(
        "acul,uacz->laz", lower_shares, output_gradient_block, preferred_element_type=jnp.float32
    )
    return (output, grad_q, grad_k, grad_v)


def shards(queries, keys, values, doc_lengths, w_out, d_out):
    rows_here = queries.shape[0]
    kv_width = keys.shape[1]
    kv_heads = kv_width // HEAD_SIZE
    queries_per_key_head = queries.shape[1] // kv_width
    reach_rows = REACH * rows_here
    window_span = reach_rows + QUERY_BLOCK_SIZE
    ext_rows = reach_rows + rows_here
    scale_factor = HEAD_SIZE ** (-0.5)
    anchor_point = lax.axis_index(("seq", "server")) * rows_here
    doc_ends = jnp.cumsum(doc_lengths)
    earlier = []
    for stride in range(REACH, 0, -1):
        earlier.append(shifted((keys, values), ("seq", "server"), stride))
    ext_keys = jnp.concatenate([pair[0] for pair in earlier] + [keys], axis=0)
    ext_values = jnp.concatenate([pair[1] for pair in earlier] + [values], axis=0)
    ext_pos = anchor_point - reach_rows + jnp.arange(ext_rows, dtype=jnp.int32)
    attention_gradient = lax.dot_general(
        d_out, w_out, (((1,), (1,)), ((), ())), preferred_element_type=jnp.float32
    ).astype(jnp.bfloat16)
    outputs = []
    grad_qs = []
    grad_k_ext = jnp.zeros((ext_rows, kv_heads, HEAD_SIZE), jnp.float32)
    grad_v_ext = jnp.zeros((ext_rows, kv_heads, HEAD_SIZE), jnp.float32)
    for block_index in range(rows_here // QUERY_BLOCK_SIZE):
        row_start = block_index * QUERY_BLOCK_SIZE
        query_block = queries[row_start : row_start + QUERY_BLOCK_SIZE].reshape(
            QUERY_BLOCK_SIZE, kv_heads, queries_per_key_head, HEAD_SIZE
        )
        output_gradient_block = attention_gradient[
            row_start : row_start + QUERY_BLOCK_SIZE
        ].reshape(QUERY_BLOCK_SIZE, kv_heads, queries_per_key_head, HEAD_SIZE)
        key_window = ext_keys[row_start : row_start + window_span].reshape(
            window_span, kv_heads, HEAD_SIZE
        )
        value_window = ext_values[row_start : row_start + window_span].reshape(
            window_span, kv_heads, HEAD_SIZE
        )
        q_pos = anchor_point + row_start + jnp.arange(QUERY_BLOCK_SIZE, dtype=jnp.int32)
        k_pos = ext_pos[row_start : row_start + window_span]
        output, grad_q, grad_k, grad_v = block_window(
            query_block,
            key_window,
            value_window,
            output_gradient_block,
            q_pos,
            k_pos,
            doc_ends,
            scale_factor,
        )
        outputs.append(output.reshape(QUERY_BLOCK_SIZE, -1))
        grad_qs.append(grad_q.astype(jnp.bfloat16).reshape(QUERY_BLOCK_SIZE, -1))
        grad_k_ext = grad_k_ext.at[row_start : row_start + window_span].add(grad_k)
        grad_v_ext = grad_v_ext.at[row_start : row_start + window_span].add(grad_v)
    attn = jnp.concatenate(outputs, axis=0)
    partial_value = jnp.dot(attn, w_out, preferred_element_type=jnp.float32).astype(jnp.bfloat16)
    attn_out = (
        lax.psum_scatter(partial_value, "tensor", scatter_dimension=1, tiled=True)
        .astype(jnp.float32)
        .astype(jnp.bfloat16)
    )
    grad_k_flat = grad_k_ext.reshape(ext_rows, kv_width)
    grad_v_flat = grad_v_ext.reshape(ext_rows, kv_width)

    def share_of(shards_back):
        row_begin = (REACH - shards_back) * rows_here
        return (
            grad_k_flat[row_begin : row_begin + rows_here],
            grad_v_flat[row_begin : row_begin + rows_here],
        )

    own_k, own_v = share_of(0)
    for stride in range(1, REACH + 1):
        partial_key, partial_value_rows = share_of(stride)
        moved_k, moved_v = (
            shifted(partial_key.astype(jnp.bfloat16), ("seq", "server"), -stride).astype(
                partial_key.dtype
            ),
            shifted(partial_value_rows.astype(jnp.bfloat16), ("seq", "server"), -stride).astype(
                partial_value_rows.dtype
            ),
        )
        own_k = own_k + moved_k
        own_v = own_v + moved_v
    grad_q_all = jnp.concatenate(grad_qs, axis=0)
    return (attn_out, grad_q_all, own_k.astype(jnp.bfloat16), own_v.astype(jnp.bfloat16))


def solution(mesh):
    return jax.shard_map(
        shards,
        mesh=mesh,
        in_specs=(
            P(("seq", "server"), "tensor"),
            P(("seq", "server"), "tensor"),
            P(("seq", "server"), "tensor"),
            P(),
            P("tensor", None),
            P(("seq", "server"), None),
        ),
        out_specs=(
            P(("seq", "server"), "tensor"),
            P(("seq", "server"), "tensor"),
            P(("seq", "server"), "tensor"),
            P(("seq", "server"), "tensor"),
        ),
        check_vma=False,
    )
```

profile of v0, /device:TPU:2, one launch (start us, length us, event | category | flops | bytes accessed | tf_op | source)
XLA Modules:
  0.0 141.6 jit_solution(17039007462210285079)
XLA Ops:
  7.2 1.8 %copy.82 = bf16[256,256]{0,1:T(8,128)(2,1)} copy(bf16[256,256]{1,0:T(8,128)(2,1)} %param.15) | data formatting | bytes 262144 | tf_op args[1]
  9.0 1.9 %collective-permute-start.7 = (bf16[256,256]{0,1:T(8,128)(2,1)}, bf16[256,256]{0,1:T(8,128)(2,1)}, u32[]{:S(2)}, u32[]{:S(2)}) collective-permute-start(bf16[256,256]{0,1:T(8,128)(2,1)} %copy.82), channel_id=1, source_target_pairs={{0,1},{1,2},{2,3},{3,16},{16,17},{17,18},{18,19},{4,5},{5,6},{6,7}... | collective-permute-start | bytes 393224 | tf_op jit(solution)/shard_map/ppermute | solution.py:14
  10.9 3.4 %collective-permute-start.6 = (bf16[256,256]{0,1:T(8,128)(2,1)}, bf16[256,256]{0,1:T(8,128)(2,1)}, u32[]{:S(2)}, u32[]{:S(2)}) collective-permute-start(bf16[256,256]{0,1:T(8,128)(2,1)} %copy.82), channel_id=1, source_target_pairs={{0,2},{1,3},{2,16},{3,17},{16,18},{17,19},{4,6},{5,7},{6,20},{7,21... | collective-permute-start | bytes 393224 | tf_op jit(solution)/shard_map/ppermute | solution.py:14
  14.4 1.9 %collective-permute-start.5 = (bf16[256,256]{0,1:T(8,128)(2,1)}, bf16[256,256]{0,1:T(8,128)(2,1)}, u32[]{:S(2)}, u32[]{:S(2)}) collective-permute-start(bf16[256,256]{0,1:T(8,128)(2,1)} %copy.82), channel_id=1, source_target_pairs={{0,3},{1,16},{2,17},{3,18},{16,19},{4,7},{5,20},{6,21},{7,22},{20,... | collective-permute-start | bytes 393224 | tf_op jit(solution)/shard_map/ppermute | solution.py:14
  16.3 1.9 %collective-permute-start.1 = (bf16[256,256]{1,0:T(8,128)(2,1)}, bf16[256,256]{1,0:T(8,128)(2,1)}, u32[]{:S(2)}, u32[]{:S(2)}) collective-permute-start(bf16[256,256]{1,0:T(8,128)(2,1)} %param.16), channel_id=1, source_target_pairs={{0,3},{1,16},{2,17},{3,18},{16,19},{4,7},{5,20},{6,21},{7,22},{20,... | collective-permute-start | bytes 393224 | tf_op jit(solution)/shard_map/ppermute | solution.py:14
  18.2 1.3 collective-permute-start
  19.6 5.7 %convolution_convert_fusion.1 = bf16[256,1024]{1,0:T(8,128)(2,1)S(1)} fusion(bf16[256,4096]{1,0:T(8,128)(2,1)S(1)} %copy-done, bf16[1024,4096]{1,0:T(8,128)(2,1)} %param.18), kind=kOutput, calls=%fused_computation.37 | convolution fusion | flops 2147745792 | bytes 11010048 | tf_op jit(solution)/shard_map/dot_general | solution.py:94
  25.8 2.3 %compare_and_fusion = (pred[128,1152]{0,1:T(8,128)(4,1)}, pred[128,1152]{0,1:T(8,128)(4,1)}) fusion(s32[128]{0:T(128)S(1)} %get-tuple-element.55, s32[128]{0:T(128)S(1)} %iota_add_fusion.1, s32[1152]{0:T(1024)S(1)} %get-tuple-element.53, s32[1152]{0:T(1024)S(1)} %get-tuple-element.76, pred[1152]{0:T(1024)(128)(4,1)S(1)} %get-tuple-element.75, ...), kind=kLoop, calls=%fused_computation.44 | loop fusion | flops 1179648 | bytes 317696 | tf_op jit(solution)/shard_map/and | solution.py:27
  28.1 1.1 fusion.39
  31.9 1.9 %collective-permute-start.2 = (bf16[256,256]{1,0:T(8,128)(2,1)}, bf16[256,256]{1,0:T(8,128)(2,1)S(1)}, u32[]{:S(2)}, u32[]{:S(2)}) collective-permute-start(bf16[256,256]{1,0:T(8,128)(2,1)} %param.16), channel_id=1, source_target_pairs={{0,2},{1,3},{2,16},{3,17},{16,18},{17,19},{4,6},{5,7},{6,20},{7,21... | collective-permute-start | bytes 393224 | tf_op jit(solution)/shard_map/ppermute | solution.py:14
  34.7 1.9 %collective-permute-start.3 = (bf16[256,256]{1,0:T(8,128)(2,1)}, bf16[256,256]{1,0:T(8,128)(2,1)S(1)}, u32[]{:S(2)}, u32[]{:S(2)}) collective-permute-start(bf16[256,256]{1,0:T(8,128)(2,1)} %param.16), channel_id=1, source_target_pairs={{0,1},{1,2},{2,3},{3,16},{16,17},{17,18},{18,19},{4,5},{5,6},{6,7}... | collective-permute-start | bytes 393224 | tf_op jit(solution)/shard_map/ppermute | solution.py:14
  36.6 0.9 constant_dynamic-update-slice_fusion.3
  37.5 3.4 %collective-permute-done.2 = bf16[256,256]{1,0:T(8,128)(2,1)S(1)} collective-permute-done((bf16[256,256]{1,0:T(8,128)(2,1)}, bf16[256,256]{1,0:T(8,128)(2,1)S(1)}, u32[]{:S(2)}, u32[]{:S(2)}) %collective-permute-start.2) | collective-permute-done | bytes 131104 | tf_op jit(solution)/shard_map/ppermute | solution.py:14
  41.0 1.5 %collective-permute-start.4 = (bf16[256,256]{0,1:T(8,128)(2,1)}, bf16[256,256]{0,1:T(8,128)(2,1)S(1)}, u32[]{:S(2)}, u32[]{:S(2)}) collective-permute-start(bf16[256,256]{0,1:T(8,128)(2,1)} %copy.82), channel_id=1, source_target_pairs={{0,16},{1,17},{2,18},{3,19},{4,20},{5,21},{6,22},{7,23},{8,24},{9,... | collective-permute-start | bytes 393224 | tf_op jit(solution)/shard_map/ppermute | solution.py:14
  42.5 0.9 constant_dynamic-update-slice_fusion
  43.4 4.6 %collective-permute-done.4 = bf16[256,256]{0,1:T(8,128)(2,1)S(1)} collective-permute-done((bf16[256,256]{0,1:T(8,128)(2,1)}, bf16[256,256]{0,1:T(8,128)(2,1)S(1)}, u32[]{:S(2)}, u32[]{:S(2)}) %collective-permute-start.4) | collective-permute-done | bytes 131104 | tf_op jit(solution)/shard_map/ppermute | solution.py:14
  48.1 0.9 constant_dynamic-update-slice_fusion.8
  49.0 0.9 constant_dynamic-update-slice_fusion.7
  50.8 0.9 constant_dynamic-update-slice_fusion.5
  51.8 1.1 fusion.34
  53.8 1.1 copy.81
  54.9 1.4 copy.91
  56.2 5.0 %exponential_reduce_fusion = (f32[2,4,128]{2,1,0:T(4,128)S(1)}, f32[2,4,128,1152]{2,3,1,0:T(8,128)}) fusion(pred[128,1152]{0,1:T(8,128)(4,1)} %get-tuple-element.88, bf16[1152,2,128,1]{0,2,3,1:T(8,128)(2,1)} %bitcast.161, bf16[128,2,4,128]{0,3,2,1:T(8,128)(2,1)} %bitcast.167), kind=kOutput, calls=%fused_computation.18 | convolution fusion | flops 306709632 | bytes 5722112 | tf_op jit(solution)/shard_map/sub | solution.py:47
  61.2 4.4 %fusion.21 = bf16[2,4,128,1152]{2,3,1,0:T(8,128)(2,1)} fusion(f32[2,4,128]{2,1,0:T(4,128)S(1)} %get-tuple-element.78, f32[2,4,128,1152]{2,3,1,0:T(8,128)} %get-tuple-element.79), kind=kLoop, calls=%fused_computation.36 | loop fusion | flops 2359296 | bytes 7081984 | tf_op jit(solution)/shard_map/convert_element_type | solution.py:49
  65.7 4.9 %exponential_reduce_fusion.1 = (f32[2,4,128]{2,1,0:T(4,128)S(1)}, f32[2,4,128,1152]{2,3,1,0:T(8,128)}) fusion(pred[128,1152]{0,1:T(8,128)(4,1)S(1)} %copy-done.18, bf16[1152,2,128,1]{0,2,3,1:T(8,128)(2,1)} %bitcast.159, bf16[128,2,4,128]{0,3,2,1:T(8,128)(2,1)S(1)} %bitcast.173), kind=kOutput, calls=%fused_computation.20 | convolution fusion | flops 306709632 | bytes 5722112 | tf_op jit(solution)/shard_map/sub | solution.py:47
  70.6 3.1 %fusion.20 = bf16[2,4,128,1152]{2,3,1,0:T(8,128)(2,1)S(1)} fusion(f32[2,4,128]{2,1,0:T(4,128)S(1)} %get-tuple-element.80, f32[2,4,128,1152]{2,3,1,0:T(8,128)} %get-tuple-element.81), kind=kLoop, calls=%fused_computation.35 | loop fusion | flops 2359296 | bytes 7081984 | tf_op jit(solution)/shard_map/convert_element_type | solution.py:49
  76.0 7.1 %convolution_convert_fusion = bf16[256,4096]{1,0:T(8,128)(2,1)} fusion(bf16[1024,4096]{1,0:T(8,128)(2,1)} %param.18, bf16[128,1024]{0,1:T(8,128)(2,1)S(1)} %bitcast.175, bf16[128,1024]{0,1:T(8,128)(2,1)S(1)} %bitcast.176), kind=kOutput, calls=%fused_computation.4 | convolution fusion | flops 2149580800 | bytes 11010048 | tf_op jit(solution)/shard_map/dot_general | solution.py:132
  83.2 4.0 %fusion.7 = bf16[2,4,128,1152]{2,3,1,0:T(8,128)(2,1)S(1)} fusion(bf16[1152,2,128,1]{0,2,3,1:T(8,128)(2,1)} %bitcast.157, bf16[128,2,4,128]{0,3,2,1:T(8,128)(2,1)} %bitcast.165, f32[2,4,128]{2,1,0:T(4,128)S(1)} %bitcast.186, f32[2,4,128]{2,1,0:T(4,128)S(1)} %get-tuple-element.80, f32[2,4,128,1152]{2,3,1,0:T(8,128)} %get-tuple-element.81), kind=kOutput, calls=%fused_computation.12 | convolution fusion | flops 306708480 | bytes 7938048 | tf_op jit(solution)/shard_map/tgrd,kgd->grtk/dot_general | solution.py:57
  88.7 1.3 fusion.5
  90.0 2.1 %fusion.33 = (bf16[1152,2,128]{0,2,1:T(8,128)(2,1)S(1)}, bf16[1280,2,128]{0,2,1:T(8,128)(2,1)S(1)}, f32[1152,2,128]{0,2,1:T(8,128)}) fusion(bf16[1280,2,128]{0,2,1:T(8,128)(2,1)S(1)} %scatter-add.14, bf16[2,4,128,1152]{2,3,1,0:T(8,128)(2,1)S(1)} %fusion.5, bf16[128,2,4,128]{0,3,2,1:T(8,128)(2,1)S(1)} %bitcast.168, f32[1152,2,128]{0,2,1:T(8,128)S(1)} %fusion.13), kind=kOutput, calls=%fused_computation.83 | convolution fusion | flops 302874624 | bytes 6750208 | tf_op jit(solution)/shard_map/acul,uacz->laz/dot_general | solution.py:66
  93.0 1.7 %copy.108 = bf16[256,256]{1,0:T(8,128)(2,1)} copy(bf16[256,256]{0,1:T(8,128)(2,1)} %bitcast.184) | data formatting | bytes 262144 | tf_op jit(solution)/shard_map/convert_element_type | solution.py:152
  96.2 0.9 slice.229
  97.9 2.5 %collective-permute-start.11 = (bf16[256,256]{1,0:T(8,128)(2,1)}, bf16[256,256]{1,0:T(8,128)(2,1)}, u32[]{:S(2)}, u32[]{:S(2)}) collective-permute-start(bf16[256,256]{1,0:T(8,128)(2,1)} %copy.112), channel_id=1, source_target_pairs={{16,0},{17,1},{18,2},{19,3},{20,4},{21,5},{22,6},{23,7},{24,8},{25... | collective-permute-start | bytes 393224 | tf_op jit(solution)/shard_map/ppermute | solution.py:14
  100.4 1.9 %collective-permute-start.9 = (bf16[256,256]{1,0:T(8,128)(2,1)}, bf16[256,256]{1,0:T(8,128)(2,1)}, u32[]{:S(2)}, u32[]{:S(2)}) collective-permute-start(bf16[256,256]{1,0:T(8,128)(2,1)} %copy.110), channel_id=1, source_target_pairs={{2,0},{3,1},{16,2},{17,3},{18,16},{19,17},{6,4},{7,5},{20,6},{21,7... | collective-permute-start | bytes 393224 | tf_op jit(solution)/shard_map/ppermute | solution.py:14
  102.3 1.9 %collective-permute-start.10 = (bf16[256,256]{1,0:T(8,128)(2,1)}, bf16[256,256]{1,0:T(8,128)(2,1)}, u32[]{:S(2)}, u32[]{:S(2)}) collective-permute-start(bf16[256,256]{1,0:T(8,128)(2,1)} %copy.111), channel_id=1, source_target_pairs={{3,0},{16,1},{17,2},{18,3},{19,16},{7,4},{20,5},{21,6},{22,7},{23,... | collective-permute-start | bytes 393224 | tf_op jit(solution)/shard_map/ppermute | solution.py:14
  104.2 1.9 %collective-permute-start.8 = (bf16[256,256]{1,0:T(8,128)(2,1)}, bf16[256,256]{1,0:T(8,128)(2,1)}, u32[]{:S(2)}, u32[]{:S(2)}) collective-permute-start(bf16[256,256]{1,0:T(8,128)(2,1)} %copy.108), channel_id=1, source_target_pairs={{1,0},{2,1},{3,2},{16,3},{17,16},{18,17},{19,18},{5,4},{6,5},{7,6}... | collective-permute-start | bytes 393224 | tf_op jit(solution)/shard_map/ppermute | solution.py:14
  106.2 2.5 %convolution_bitcast_fusion.1 = f32[1152,2,128]{0,2,1:T(8,128)S(1)} fusion(bf16[128,2,4,128]{0,3,2,1:T(8,128)(2,1)S(1)} %bitcast.166, bf16[2,4,128,1152]{2,3,1,0:T(8,128)(2,1)} %copy-done.3), kind=kOutput, calls=%fused_computation.23 | convolution fusion | flops 301989888 | bytes 3801088 | tf_op jit(solution)/shard_map/acul,uacz->laz/dot_general | solution.py:71
  109.4 1.0 copy-done.7
  111.0 1.1 copy-done.2
  112.2 1.9 %fusion.32 = (bf16[1152,2,128]{0,2,1:T(8,128)(2,1)S(1)}, bf16[1280,2,128]{0,2,1:T(8,128)(2,1)S(1)}, f32[1152,2,128]{0,2,1:T(8,128)}) fusion(bf16[1280,2,128]{0,2,1:T(8,128)(2,1)S(1)} %scatter-add.16, bf16[128,2,4,128]{0,3,2,1:T(8,128)(2,1)S(1)} %bitcast.164, bf16[2,4,128,1152]{2,3,1,0:T(8,128)(2,1)S(1)} %copy-done.2, ...), kind=kOutput, calls=%fused_computation.82 | convolution fusion | flops 302579712 | bytes 6750208 | tf_op jit(solution)/shard_map/acul,uacz->laz/dot_general | solution.py:71
  115.3 1.0 slice.212
  120.3 1.3 collective-permute-start.15
  121.6 1.0 slice.217
  123.5 1.9 %collective-permute-start.13 = (bf16[256,256]{1,0:T(8,128)(2,1)}, bf16[256,256]{1,0:T(8,128)(2,1)S(1)}, u32[]{:S(2)}, u32[]{:S(2)}) collective-permute-start(bf16[256,256]{1,0:T(8,128)(2,1)} %copy.117), channel_id=1, source_target_pairs={{2,0},{3,1},{16,2},{17,3},{18,16},{19,17},{6,4},{7,5},{20,6},{21,7... | collective-permute-start | bytes 393224 | tf_op jit(solution)/shard_map/ppermute | solution.py:14
  125.5 1.9 %collective-permute-start.14 = (bf16[256,256]{1,0:T(8,128)(2,1)}, bf16[256,256]{1,0:T(8,128)(2,1)S(1)}, u32[]{:S(2)}, u32[]{:S(2)}) collective-permute-start(bf16[256,256]{1,0:T(8,128)(2,1)} %copy.118), channel_id=1, source_target_pairs={{3,0},{16,1},{17,2},{18,3},{19,16},{7,4},{20,5},{21,6},{22,7},{23,... | collective-permute-start | bytes 393224 | tf_op jit(solution)/shard_map/ppermute | solution.py:14
  127.4 1.9 %collective-permute-start.12 = (bf16[256,256]{1,0:T(8,128)(2,1)}, bf16[256,256]{1,0:T(8,128)(2,1)S(1)}, u32[]{:S(2)}, u32[]{:S(2)}) collective-permute-start(bf16[256,256]{1,0:T(8,128)(2,1)} %copy.115), channel_id=1, source_target_pairs={{1,0},{2,1},{3,2},{16,3},{17,16},{18,17},{19,18},{5,4},{6,5},{7,6}... | collective-permute-start | bytes 393224 | tf_op jit(solution)/shard_map/ppermute | solution.py:14
  129.3 1.8 %add_convert_fusion.1 = bf16[256,256]{1,0:T(8,128)(2,1)} fusion(bf16[256,256]{1,0:T(8,128)(2,1)} %collective-permute-done.11, bf16[256,256]{1,0:T(8,128)(2,1)} %collective-permute-done.10, bf16[256,256]{1,0:T(8,128)(2,1)} %collective-permute-done.9, f32[256,256]{1,0:T(8,128)S(1)} %copy.109, bf16[256,256]{1,0:T(8,128)(2,1)} %collective-permute-done.8), kind=kLoop, calls=%fused_computation.55 | loop fusion | flops 589824 | bytes 917504 | tf_op jit(solution)/shard_map/convert_element_type | solution.py:162
  131.7 2.3 %collective-permute-done.14 = bf16[256,256]{1,0:T(8,128)(2,1)S(1)} collective-permute-done((bf16[256,256]{1,0:T(8,128)(2,1)}, bf16[256,256]{1,0:T(8,128)(2,1)S(1)}, u32[]{:S(2)}, u32[]{:S(2)}) %collective-permute-start.14) | collective-permute-done | bytes 131104 | tf_op jit(solution)/shard_map/ppermute | solution.py:14
  (101 shorter events, 21.5 us)
Async XLA Ops:
  7.2 12.5 %copy-start = (bf16[256,4096]{1,0:T(8,128)(2,1)S(1)}, bf16[256,4096]{1,0:T(8,128)(2,1)}, u32[]{:S(2)}) copy-start(bf16[256,4096]{1,0:T(8,128)(2,1)} %param.19) | copy-start | bytes 6291460
  7.2 127.5 %reduce-scatter.2.cloned.1.call-start = ((), (), s32[]{:S(2)}) async-start(), calls=%async_computation.1 | async-start | bytes 2621440 | tf_op jit(solution)/shard_map/reduce_scatter | solution.py:134
  9.0 40.9 %collective-permute-start.7 = (bf16[256,256]{0,1:T(8,128)(2,1)}, bf16[256,256]{0,1:T(8,128)(2,1)}, u32[]{:S(2)}, u32[]{:S(2)}) collective-permute-start(bf16[256,256]{0,1:T(8,128)(2,1)} %copy.82), channel_id=1, source_target_pairs={{0,1},{1,2},{2,3},{3,16},{16,17},{17,18},{18,19},{4,5},{5,6},{6,7}... | collective-permute-start | bytes 393224 | tf_op jit(solution)/shard_map/ppermute | solution.py:14
  10.9 38.0 %collective-permute-start.6 = (bf16[256,256]{0,1:T(8,128)(2,1)}, bf16[256,256]{0,1:T(8,128)(2,1)}, u32[]{:S(2)}, u32[]{:S(2)}) collective-permute-start(bf16[256,256]{0,1:T(8,128)(2,1)} %copy.82), channel_id=1, source_target_pairs={{0,2},{1,3},{2,16},{3,17},{16,18},{17,19},{4,6},{5,7},{6,20},{7,21... | collective-permute-start | bytes 393224 | tf_op jit(solution)/shard_map/ppermute | solution.py:14
  14.4 33.7 %collective-permute-start.5 = (bf16[256,256]{0,1:T(8,128)(2,1)}, bf16[256,256]{0,1:T(8,128)(2,1)}, u32[]{:S(2)}, u32[]{:S(2)}) collective-permute-start(bf16[256,256]{0,1:T(8,128)(2,1)} %copy.82), channel_id=1, source_target_pairs={{0,3},{1,16},{2,17},{3,18},{16,19},{4,7},{5,20},{6,21},{7,22},{20,... | collective-permute-start | bytes 393224 | tf_op jit(solution)/shard_map/ppermute | solution.py:14
  16.3 18.4 %collective-permute-start.1 = (bf16[256,256]{1,0:T(8,128)(2,1)}, bf16[256,256]{1,0:T(8,128)(2,1)}, u32[]{:S(2)}, u32[]{:S(2)}) collective-permute-start(bf16[256,256]{1,0:T(8,128)(2,1)} %param.16), channel_id=1, source_target_pairs={{0,3},{1,16},{2,17},{3,18},{16,19},{4,7},{5,20},{6,21},{7,22},{20,... | collective-permute-start | bytes 393224 | tf_op jit(solution)/shard_map/ppermute | solution.py:14
  18.2 13.6 %collective-permute-start = (bf16[256,256]{1,0:T(8,128)(2,1)}, bf16[256,256]{1,0:T(8,128)(2,1)}, u32[]{:S(2)}, u32[]{:S(2)}) collective-permute-start(bf16[256,256]{1,0:T(8,128)(2,1)} %param.16), channel_id=1, source_target_pairs={{0,16},{1,17},{2,18},{3,19},{4,20},{5,21},{6,22},{7,23},{8,24},{9,... | collective-permute-start | bytes 393224 | tf_op jit(solution)/shard_map/ppermute | solution.py:14
  19.6 5.8 %copy-start.19 = (s32[4]{0:T(128)S(1)}, s32[4]{0:T(128)}, u32[]{:S(2)}) copy-start(s32[4]{0:T(128)} %param.17) | copy-start | bytes 52
  31.9 9.1 %collective-permute-start.2 = (bf16[256,256]{1,0:T(8,128)(2,1)}, bf16[256,256]{1,0:T(8,128)(2,1)S(1)}, u32[]{:S(2)}, u32[]{:S(2)}) collective-permute-start(bf16[256,256]{1,0:T(8,128)(2,1)} %param.16), channel_id=1, source_target_pairs={{0,2},{1,3},{2,16},{3,17},{16,18},{17,19},{4,6},{5,7},{6,20},{7,21... | collective-permute-start | bytes 393224 | tf_op jit(solution)/shard_map/ppermute | solution.py:14
  34.7 7.8 %collective-permute-start.3 = (bf16[256,256]{1,0:T(8,128)(2,1)}, bf16[256,256]{1,0:T(8,128)(2,1)S(1)}, u32[]{:S(2)}, u32[]{:S(2)}) collective-permute-start(bf16[256,256]{1,0:T(8,128)(2,1)} %param.16), channel_id=1, source_target_pairs={{0,1},{1,2},{2,3},{3,16},{16,17},{17,18},{18,19},{4,5},{5,6},{6,7}... | collective-permute-start | bytes 393224 | tf_op jit(solution)/shard_map/ppermute | solution.py:14
  41.0 7.1 %collective-permute-start.4 = (bf16[256,256]{0,1:T(8,128)(2,1)}, bf16[256,256]{0,1:T(8,128)(2,1)S(1)}, u32[]{:S(2)}, u32[]{:S(2)}) collective-permute-start(bf16[256,256]{0,1:T(8,128)(2,1)} %copy.82), channel_id=1, source_target_pairs={{0,16},{1,17},{2,18},{3,19},{4,20},{5,21},{6,22},{7,23},{8,24},{9,... | collective-permute-start | bytes 393224 | tf_op jit(solution)/shard_map/ppermute | solution.py:14
  61.2 4.4 %copy-start.14 = (bf16[128,1024]{0,1:T(8,128)(2,1)S(1)}, bf16[128,1024]{0,1:T(8,128)(2,1)}, u32[]{:S(2)}) copy-start(bf16[128,1024]{0,1:T(8,128)(2,1)} %copy.152) | copy-start | bytes 786436
  61.2 4.4 %copy-start.18 = (pred[128,1152]{0,1:T(8,128)(4,1)S(1)}, pred[128,1152]{0,1:T(8,128)(4,1)}, u32[]{:S(2)}) copy-start(pred[128,1152]{0,1:T(8,128)(4,1)} %get-tuple-element.89) | copy-start | bytes 442372
  70.6 3.1 %copy-start.1 = (bf16[2,4,128,1152]{2,3,1,0:T(8,128)(2,1)S(1)}, bf16[2,4,128,1152]{2,3,1,0:T(8,128)(2,1)}, u32[]{:S(2)}) copy-start(bf16[2,4,128,1152]{2,3,1,0:T(8,128)(2,1)} %fusion.21) | copy-start | bytes 7077892
  73.7 2.3 %copy-start.3 = (bf16[2,4,128,1152]{2,3,1,0:T(8,128)(2,1)}, bf16[2,4,128,1152]{2,3,1,0:T(8,128)(2,1)S(1)}, u32[]{:S(2)}) copy-start(bf16[2,4,128,1152]{2,3,1,0:T(8,128)(2,1)S(1)} %fusion.20) | copy-start | bytes 7077892
  73.7 1.5 %copy-start.8 = (bf16[1152,256]{0,1:T(8,128)(2,1)S(1)}, bf16[1152,256]{0,1:T(8,128)(2,1)}, u32[]{:S(2)}) copy-start(bf16[1152,256]{0,1:T(8,128)(2,1)} %copy.81) | copy-start | bytes 1769476
  73.7 1.7 %copy-start.11 = (bf16[128,1024]{0,1:T(8,128)(2,1)S(1)}, bf16[128,1024]{0,1:T(8,128)(2,1)}, u32[]{:S(2)}) copy-start(bf16[128,1024]{0,1:T(8,128)(2,1)} %copy.96) | copy-start | bytes 786436
  83.1 5.5 %slice-start = ((s8[4718592]{0:T(1024)(128)(4,1)}), s8[524288]{0:T(1024)(128)(4,1)S(1)}, s32[]{:S(2)}) async-start(s8[4718592]{0:T(1024)(128)(4,1)} %bitcast.153), calls=%async_computation.2 | async-start | bytes 1048576
  83.1 4.1 %copy-start.15 = (bf16[128,1024]{0,1:T(8,128)(2,1)S(1)}, bf16[128,1024]{0,1:T(8,128)(2,1)}, u32[]{:S(2)}) copy-start(bf16[128,1024]{0,1:T(8,128)(2,1)} %copy.152) | copy-start | bytes 786436
  83.1 5.5 %slice-start.1 = ((s8[4718592]{0:T(1024)(128)(4,1)}), s8[4194304]{0:T(1024)(128)(4,1)S(1)}, s32[]{:S(2)}) async-start(s8[4718592]{0:T(1024)(128)(4,1)} %bitcast.153), calls=%async_computation.3 | async-start | bytes 8388608
  87.2 1.4 %copy-start.6 = (bf16[2,4,128,1152]{2,3,1,0:T(8,128)(2,1)}, bf16[2,4,128,1152]{2,3,1,0:T(8,128)(2,1)S(1)}, u32[]{:S(2)}) copy-start(bf16[2,4,128,1152]{2,3,1,0:T(8,128)(2,1)S(1)} %fusion.7) | copy-start | bytes 7077892
  88.7 1.3 copy-start.13
  90.0 2.1 %copy-start.4 = (bf16[2,4,128,1152]{2,3,1,0:T(8,128)(2,1)}, bf16[2,4,128,1152]{2,3,1,0:T(8,128)(2,1)S(1)}, u32[]{:S(2)}) copy-start(bf16[2,4,128,1152]{2,3,1,0:T(8,128)(2,1)S(1)} %fusion.5) | copy-start | bytes 7077892
  90.0 16.2 %copy-start.12 = (bf16[128,1024]{0,1:T(8,128)(2,1)S(1)}, bf16[128,1024]{0,1:T(8,128)(2,1)}, u32[]{:S(2)}) copy-start(bf16[128,1024]{0,1:T(8,128)(2,1)} %copy.96) | copy-start | bytes 786436
  92.1 0.9 copy-start.17
  97.9 11.0 %copy-start.5 = (bf16[2,4,128,1152]{2,3,1,0:T(8,128)(2,1)S(1)}, bf16[2,4,128,1152]{2,3,1,0:T(8,128)(2,1)}, u32[]{:S(2)}) copy-start(bf16[2,4,128,1152]{2,3,1,0:T(8,128)(2,1)} %copy-done.4) | copy-start | bytes 7077892
  97.9 11.0 %copy-start.10 = (bf16[1152,256]{0,1:T(8,128)(2,1)S(1)}, bf16[1152,256]{0,1:T(8,128)(2,1)}, u32[]{:S(2)}) copy-start(bf16[1152,256]{0,1:T(8,128)(2,1)} %get-tuple-element.61) | copy-start | bytes 1769476
  97.9 25.7 %collective-permute-start.11 = (bf16[256,256]{1,0:T(8,128)(2,1)}, bf16[256,256]{1,0:T(8,128)(2,1)}, u32[]{:S(2)}, u32[]{:S(2)}) collective-permute-start(bf16[256,256]{1,0:T(8,128)(2,1)} %copy.112), channel_id=1, source_target_pairs={{16,0},{17,1},{18,2},{19,3},{20,4},{21,5},{22,6},{23,7},{24,8},{25... | collective-permute-start | bytes 393224 | tf_op jit(solution)/shard_map/ppermute | solution.py:14
  100.4 25.1 %collective-permute-start.9 = (bf16[256,256]{1,0:T(8,128)(2,1)}, bf16[256,256]{1,0:T(8,128)(2,1)}, u32[]{:S(2)}, u32[]{:S(2)}) collective-permute-start(bf16[256,256]{1,0:T(8,128)(2,1)} %copy.110), channel_id=1, source_target_pairs={{2,0},{3,1},{16,2},{17,3},{18,16},{19,17},{6,4},{7,5},{20,6},{21,7... | collective-permute-start | bytes 393224 | tf_op jit(solution)/shard_map/ppermute | solution.py:14
  102.3 25.1 %collective-permute-start.10 = (bf16[256,256]{1,0:T(8,128)(2,1)}, bf16[256,256]{1,0:T(8,128)(2,1)}, u32[]{:S(2)}, u32[]{:S(2)}) collective-permute-start(bf16[256,256]{1,0:T(8,128)(2,1)} %copy.111), channel_id=1, source_target_pairs={{3,0},{16,1},{17,2},{18,3},{19,16},{7,4},{20,5},{21,6},{22,7},{23,... | collective-permute-start | bytes 393224 | tf_op jit(solution)/shard_map/ppermute | solution.py:14
  104.2 25.1 %collective-permute-start.8 = (bf16[256,256]{1,0:T(8,128)(2,1)}, bf16[256,256]{1,0:T(8,128)(2,1)}, u32[]{:S(2)}, u32[]{:S(2)}) collective-permute-start(bf16[256,256]{1,0:T(8,128)(2,1)} %copy.108), channel_id=1, source_target_pairs={{1,0},{2,1},{3,2},{16,3},{17,16},{18,17},{19,18},{5,4},{6,5},{7,6}... | collective-permute-start | bytes 393224 | tf_op jit(solution)/shard_map/ppermute | solution.py:14
  108.7 1.7 %copy-start.7 = (bf16[2,4,128,1152]{2,3,1,0:T(8,128)(2,1)S(1)}, bf16[2,4,128,1152]{2,3,1,0:T(8,128)(2,1)}, u32[]{:S(2)}) copy-start(bf16[2,4,128,1152]{2,3,1,0:T(8,128)(2,1)} %copy-done.6) | copy-start | bytes 7077892
  108.7 1.8 %copy-start.9 = (bf16[1152,256]{0,1:T(8,128)(2,1)S(1)}, bf16[1152,256]{0,1:T(8,128)(2,1)}, u32[]{:S(2)}) copy-start(bf16[1152,256]{0,1:T(8,128)(2,1)} %get-tuple-element.60) | copy-start | bytes 1769476
  110.5 1.7 %copy-start.2 = (bf16[2,4,128,1152]{2,3,1,0:T(8,128)(2,1)S(1)}, bf16[2,4,128,1152]{2,3,1,0:T(8,128)(2,1)}, u32[]{:S(2)}) copy-start(bf16[2,4,128,1152]{2,3,1,0:T(8,128)(2,1)} %fusion.21) | copy-start | bytes 7077892
  114.1 0.8 copy-start.16
  120.3 10.9 %collective-permute-start.15 = (bf16[256,256]{1,0:T(8,128)(2,1)}, bf16[256,256]{1,0:T(8,128)(2,1)S(1)}, u32[]{:S(2)}, u32[]{:S(2)}) collective-permute-start(bf16[256,256]{1,0:T(8,128)(2,1)} %copy.119), channel_id=1, source_target_pairs={{16,0},{17,1},{18,2},{19,3},{20,4},{21,5},{22,6},{23,7},{24,8},{25... | collective-permute-start | bytes 393224 | tf_op jit(solution)/shard_map/ppermute | solution.py:14
  123.5 8.1 %collective-permute-start.13 = (bf16[256,256]{1,0:T(8,128)(2,1)}, bf16[256,256]{1,0:T(8,128)(2,1)S(1)}, u32[]{:S(2)}, u32[]{:S(2)}) collective-permute-start(bf16[256,256]{1,0:T(8,128)(2,1)} %copy.117), channel_id=1, source_target_pairs={{2,0},{3,1},{16,2},{17,3},{18,16},{19,17},{6,4},{7,5},{20,6},{21,7... | collective-permute-start | bytes 393224 | tf_op jit(solution)/shard_map/ppermute | solution.py:14
  125.5 8.5 %collective-permute-start.14 = (bf16[256,256]{1,0:T(8,128)(2,1)}, bf16[256,256]{1,0:T(8,128)(2,1)S(1)}, u32[]{:S(2)}, u32[]{:S(2)}) collective-permute-start(bf16[256,256]{1,0:T(8,128)(2,1)} %copy.118), channel_id=1, source_target_pairs={{3,0},{16,1},{17,2},{18,3},{19,16},{7,4},{20,5},{21,6},{22,7},{23,... | collective-permute-start | bytes 393224 | tf_op jit(solution)/shard_map/ppermute | solution.py:14
  127.4 6.6 %collective-permute-start.12 = (bf16[256,256]{1,0:T(8,128)(2,1)}, bf16[256,256]{1,0:T(8,128)(2,1)S(1)}, u32[]{:S(2)}, u32[]{:S(2)}) collective-permute-start(bf16[256,256]{1,0:T(8,128)(2,1)} %copy.115), channel_id=1, source_target_pairs={{1,0},{2,1},{3,2},{16,3},{17,16},{18,17},{19,18},{5,4},{6,5},{7,6}... | collective-permute-start | bytes 393224 | tf_op jit(solution)/shard_map/ppermute | solution.py:14
Sparse Core Ops, SparseCore 0:
  83.3 43.8 reduce-scatter.1
where the time goes:
time: 144 us; the launch traced here: 142 us
  matrix products  37.7 us (26%)
  local copies, waits for them, and re-layouts  33.6 us (23%)
  starting transfers between devices  31.1 us (22%)
  between operations  14.6 us (10%)
  other arithmetic  13.6 us (9%)
  waiting for transfers between devices  10.9 us (8%)
    ppermute x16, starting transfers between devices, shifted(): return lax.ppermute(block, axis, route)  31.1 us
    unnamed x55, local copies, waits for them, and re-layouts  13.1 us
    ppermute x16, waiting for transfers between devices, shifted(): return lax.ppermute(block, axis, route)  10.9 us
    sub x2, matrix products, block_window(): weights = jnp.exp(masked - row_top)  9.97 us
    convert_element_type x2, other arithmetic, block_window(): lower_shares = shares.astype(jnp.bfloat16)  7.51 us
    dot_general x1, matrix products, shards(): jnp.dot(attn, w_out, preferred_element_type=jnp.float32)  7.07 us
    dot_general x1, matrix products, shards(): lax.dot_general(d_out, w_out, (((1,), (1,)), ((), ())), preferred_element...  5.74 us
    dot_general x2, matrix products, block_window(): jnp.einsum('tgrd,kgd->grtk', output_gradient_block, value_window, preferr...  5.33 us
  transfers between devices with their start and end apart: 17, of which 4 were waited for; matrix products, arithmetic and copies ran while one was open for 33% of the time, Pallas kernels for 0%

commit v1 on v0

v1 whole, which is shorter than its diff:
```python
import functools
import math

import jax
import jax.numpy as jnp
from jax import lax
from jax.experimental import pallas as pl
from jax.experimental.pallas import tpu as pltpu
from jax.sharding import PartitionSpec as P

HEAD = 128
REACH = 4
CHUNKS = 2
ROW_BLOCK = 32
MESH = pl.DeviceIdType.MESH
NT = (((1,), (1,)), ((), ()))
TN = (((0,), (0,)), ((), ()))


def dot(a, b, dims=(((1,), (0,)), ((), ()))):
    return lax.dot_general(a, b, dims, preferred_element_type=jnp.float32)


def kernel(
    sizes,
    q_hbm, k_hbm, v_hbm, doc, w_hbm, do_hbm,
    out_ref, gq_ref, gk_ref, gv_ref,
    q_in, do_in, w, kx, vx, qs, dos, attn, bias, s_ref, p_ref, delta,
    dp_ref, ds_ref, dq_acc, gsk, gsv, grk, grv, gown, part, rr, rl,
    loc_sem, w_sem, kv_send, kv_recv, fw_send, fw_recv, g_send, g_recv,
    r_send, r_recv, l_send, l_recv,
):
    n_seq, n_server, n_t = sizes
    n_shards = n_seq * n_server
    rows = q_in.shape[0]
    heads = q_in.shape[1] // HEAD
    groups = kx.shape[1] // HEAD
    per = heads // groups
    chunk = rows // CHUNKS
    ext = kx.shape[0]
    reach_rows = REACH * rows
    window = reach_rows + chunk
    crows = per * chunk
    width = out_ref.shape[1]
    scale = HEAD ** -0.5

    shard = lax.axis_index("seq") * n_server + lax.axis_index("server")
    t = lax.axis_index("tensor")

    def at_shard(other):
        return {"seq": other // n_server, "server": lax.rem(other, n_server)}

    loads = [
        pltpu.make_async_copy(k_hbm, kx.at[pl.ds(reach_rows, rows)], loc_sem.at[0]),
        pltpu.make_async_copy(v_hbm, vx.at[pl.ds(reach_rows, rows)], loc_sem.at[1]),
        pltpu.make_async_copy(do_hbm, do_in, loc_sem.at[2]),
        pltpu.make_async_copy(q_hbm, q_in, loc_sem.at[3]),
    ]
    n_w = w_sem.shape[0]
    w_rows = w.shape[0] // n_w
    w_loads = [
        pltpu.make_async_copy(
            w_hbm.at[pl.ds(j * w_rows, w_rows)], w.at[pl.ds(j * w_rows, w_rows)], w_sem.at[j]
        )
        for j in range(n_w)
    ]
    for c in loads:
        c.start()
    for c in w_loads:
        c.start()

    barrier = pltpu.get_barrier_semaphore()
    count = jnp.int32(0)
    for step in range(1, REACH + 1):
        for sign in (1, -1):
            other = shard + sign * step
            ok = (other >= 0) & (other < n_shards)

            @pl.when(ok)
            def _():
                pl.semaphore_signal(barrier, inc=1, device_id=at_shard(other), device_id_type=MESH)

            count = count + ok.astype(jnp.int32)
    for sign in (1, -1):
        other = t + sign
        ok = (other >= 0) & (other < n_t)

        @pl.when(ok)
        def _():
            pl.semaphore_signal(barrier, inc=1, device_id={"tensor": other}, device_id_type=MESH)

        count = count + ok.astype(jnp.int32)
    pl.semaphore_wait(barrier, count)

    def slot(distance):
        return pl.ds((REACH - distance) * rows, rows)

    def kv_copy(i, distance):
        src, dst = ((k_hbm, kx), (v_hbm, vx))[i]
        e = 2 * (distance // 2 - 1) + i
        return pltpu.make_async_remote_copy(
            src_ref=src,
            dst_ref=dst.at[slot(distance)],
            send_sem=kv_send.at[e],
            recv_sem=kv_recv.at[e],
            device_id=at_shard(shard + distance),
            device_id_type=MESH,
        )

    even = lax.rem(shard, 2) == 0
    partner = shard + 1 - 2 * lax.rem(shard, 2)

    def fw_copy(i, from_distance, to_distance):
        ref = (kx, vx)[i]
        e = 2 * (to_distance // 2) + i
        return pltpu.make_async_remote_copy(
            src_ref=ref.at[slot(from_distance)],
            dst_ref=ref.at[slot(to_distance)],
            send_sem=fw_send.at[e],
            recv_sem=fw_recv.at[e],
            device_id=at_shard(partner),
            device_id_type=MESH,
        )

    for distance in (4, 2):

        @pl.when(shard + distance < n_shards)
        def _():
            for i in range(2):
                kv_copy(i, distance).start()

    for c in loads[:2]:
        c.wait()

    @pl.when(even)
    def _():
        for i in range(2):
            fw_copy(i, 0, 1).start()

    for distance in range(1, REACH + 1):

        @pl.when(shard < distance)
        def _():
            kx[slot(distance)] = jnp.zeros((rows, kx.shape[1]), kx.dtype)
            vx[slot(distance)] = jnp.zeros((rows, kx.shape[1]), kx.dtype)

    loads[2].wait()
    loads[3].wait()
    heads_per_w = w_rows // HEAD
    for j in range(n_w):
        w_loads[j].wait()
        d = dot(do_in[...], w[pl.ds(j * w_rows, w_rows)], NT).astype(jnp.bfloat16)
        for a in range(heads_per_w):
            h = j * heads_per_w + a
            g, r = h // per, h % per
            for c in range(CHUNKS):
                place = pl.ds(c * crows + r * chunk, chunk)
                dos[g, place] = d[c * chunk : (c + 1) * chunk, a * HEAD : (a + 1) * HEAD]
                qs[g, place] = q_in[pl.ds(c * chunk, chunk), pl.ds(h * HEAD, HEAD)]

    for c in range(CHUNKS):
        first = shard * rows + c * chunk
        q_pos = first + lax.broadcasted_iota(jnp.int32, (chunk, 1), 0)
        start = jnp.zeros((chunk, 1), jnp.int32)
        end = jnp.int32(0)
        for a in range(doc.shape[0]):
            end = end + doc[a]
            start = jnp.maximum(start, jnp.where(end <= q_pos, end, 0))
        k_pos = first - reach_rows + lax.broadcasted_iota(jnp.int32, (chunk, window), 1)
        bias[c] = jnp.where((k_pos >= start) & (k_pos <= q_pos), 0.0, -1e30).astype(jnp.float32)
    if CHUNKS > 1:
        for g in range(groups):
            for c in range(CHUNKS):
                place = pl.ds(c * crows, crows)
                if c > 0:
                    p_ref[g, place, pl.ds(0, c * chunk)] = jnp.zeros((crows, c * chunk), jnp.bfloat16)
                tail = ext - window - c * chunk
                if tail > 0:
                    p_ref[g, place, pl.ds(ext - tail, tail)] = jnp.zeros((crows, tail), jnp.bfloat16)

    @pl.when(shard >= 2)
    def _():
        for i in range(2):
            kv_copy(i, 2).wait_recv()

        @pl.when(even)
        def _():
            for i in range(2):
                fw_copy(i, 2, 3).start()

        @pl.when(jnp.logical_not(even))
        def _():
            for i in range(2):
                fw_copy(i, 2, 1).start()

    @pl.when(shard >= 4)
    def _():
        for i in range(2):
            kv_copy(i, 4).wait_recv()

        @pl.when(jnp.logical_not(even))
        def _():
            for i in range(2):
                fw_copy(i, 4, 3).start()

    @pl.when(shard >= 1)
    def _():
        for i in range(2):
            fw_copy(i, 0, 1).wait_recv()

    @pl.when(shard >= 3)
    def _():
        for i in range(2):
            fw_copy(i, 2, 3).wait_recv()

    order = []
    for a in range((n_t + 1) // 2):
        order.append(n_t - 1 - a)
        if a != n_t - 1 - a:
            order.append(a)

    def cols(d):
        return pl.ds(d * width, width)

    def right_copy(c, d):
        return pltpu.make_async_remote_copy(
            src_ref=part.at[c, d],
            dst_ref=rr.at[c, d],
            send_sem=r_send.at[c, d],
            recv_sem=r_recv.at[c, d],
            device_id={"tensor": t + 1},
            device_id_type=MESH,
        )

    def left_copy(c, d):
        return pltpu.make_async_remote_copy(
            src_ref=part.at[c, d],
            dst_ref=rl.at[c, d],
            send_sem=l_send.at[c, d],
            recv_sem=l_recv.at[c, d],
            device_id={"tensor": t - 1},
            device_id_type=MESH,
        )

    def relay(c, d):
        e = n_t - 1 - d
        if d > 0:

            @pl.when((t > 0) & (t < d))
            def _():
                right_copy(c, d).wait_recv()
                part[c, d] = (part[c, d].astype(jnp.float32) + rr[c, d].astype(jnp.float32)).astype(
                    jnp.bfloat16
                )
                right_copy(c, d).start()

            @pl.when((t < n_t - 1) & (t > e))
            def _():
                left_copy(c, e).wait_recv()
                part[c, e] = (part[c, e].astype(jnp.float32) + rl[c, e].astype(jnp.float32)).astype(
                    jnp.bfloat16
                )
                left_copy(c, e).start()

    factor = scale * math.log2(math.e)
    blocks = crows // ROW_BLOCK
    per_head = chunk // ROW_BLOCK
    for c in range(CHUNKS):
        place = pl.ds(c * crows, crows)
        win = pl.ds(c * chunk, window)
        for g in range(groups):
            gc = pl.ds(g * HEAD, HEAD)
            s_ref[...] = dot(qs[g, place], kx[win, gc], NT)

            @pl.loop(0, blocks, unroll=2)
            def _(b):
                row = pl.multiple_of(b * ROW_BLOCK, ROW_BLOCK)
                brow = pl.multiple_of(lax.rem(b, per_head) * ROW_BLOCK, ROW_BLOCK)
                s = s_ref[pl.ds(row, ROW_BLOCK)] + bias[c, pl.ds(brow, ROW_BLOCK)]
                top = jnp.max(s, axis=1, keepdims=True)
                e = jnp.exp2((s - top) * factor)
                inv = 1.0 / jnp.sum(e, axis=1, keepdims=True)
                p_ref[g, pl.ds(c * crows + row, ROW_BLOCK), win] = (e * inv).astype(jnp.bfloat16)

            o = dot(p_ref[g, place, win], vx[win, gc]).astype(jnp.bfloat16)
            delta[g, place] = jnp.sum(
                o.astype(jnp.float32) * dos[g, place].astype(jnp.float32), axis=1, keepdims=True
            )
            for r in range(per):
                attn[c, :, pl.ds((g * per + r) * HEAD, HEAD)] = o[r * chunk : (r + 1) * chunk]
        for d in order:
            part[c, d] = dot(attn[c], w[:, cols(d)]).astype(jnp.bfloat16)
            if d > 0:

                @pl.when(t == 0)
                def _():
                    right_copy(c, d).start()

            if d < n_t - 1:

                @pl.when(t == n_t - 1)
                def _():
                    left_copy(c, d).start()

    def grad_copy(i, distance):
        src, dst = ((gsk, grk), (gsv, grv))[i]
        return pltpu.make_async_remote_copy(
            src_ref=src.at[distance - 1],
            dst_ref=dst.at[distance - 1],
            send_sem=g_send.at[i, distance - 1],
            recv_sem=g_recv.at[i, distance - 1],
            device_id=at_shard(shard - distance),
            device_id_type=MESH,
        )

    for kb in range(REACH + 1):
        distance = REACH - kb
        keys = pl.ds(kb * rows, rows)
        for g in range(groups):
            gc = pl.ds(g * HEAD, HEAD)
            dp_ref[...] = dot(dos[g], vx[keys, gc], NT)
            ds_ref[...] = (p_ref[g, :, keys].astype(jnp.float32) * (dp_ref[...] - delta[g])).astype(
                jnp.bfloat16
            )
            dq = dot(ds_ref[...], kx[keys, gc])
            if kb == 0:
                dq_acc[g] = dq
            else:
                dq_acc[g] += dq
            dk = dot(ds_ref[...], qs[g], TN) * scale
            dv = dot(p_ref[g, :, keys], dos[g], TN)
            if distance > 0:
                gsk[distance - 1, :, gc] = dk.astype(jnp.bfloat16)
                gsv[distance - 1, :, gc] = dv.astype(jnp.bfloat16)
            else:
                gown[0, :, gc] = dk
                gown[1, :, gc] = dv
        if distance > 0:

            @pl.when(shard >= distance)
            def _():
                for i in range(2):
                    grad_copy(i, distance).start()

        if kb == 2:
            relay(0, n_t - 1)
        if kb == 4:
            for d in range(n_t - 2, 0, -1):
                relay(0, d)

    for g in range(groups):
        for c in range(CHUNKS):
            for r in range(per):
                gq_ref[pl.ds(c * chunk, chunk), pl.ds((g * per + r) * HEAD, HEAD)] = (
                    dq_acc[g, pl.ds(c * crows + r * chunk, chunk)] * scale
                ).astype(jnp.bfloat16)

    for c in range(1, CHUNKS):
        for d in range(n_t - 1, 0, -1):
            relay(c, d)

    for distance in range(REACH, 0, -1):

        @pl.when(shard + distance < n_shards)
        def _():
            for i, ref in enumerate((grk, grv)):
                grad_copy(i, distance).wait_recv()
                gown[i] += ref[distance - 1].astype(jnp.float32)

    gk_ref[...] = gown[0].astype(jnp.bfloat16)
    gv_ref[...] = gown[1].astype(jnp.bfloat16)

    for c in range(CHUNKS):
        here = pl.ds(c * chunk, chunk)
        for d in range(n_t):

            @pl.when(t == d)
            def _():
                total = part[c, d].astype(jnp.float32)
                if d > 0:
                    right_copy(c, d).wait_recv()
                    total = total + rr[c, d].astype(jnp.float32)
                if d < n_t - 1:
                    left_copy(c, d).wait_recv()
                    total = total + rl[c, d].astype(jnp.float32)
                out_ref[here] = total.astype(jnp.bfloat16)

    for distance in (4, 2):

        @pl.when(shard + distance < n_shards)
        def _():
            for i in range(2):
                kv_copy(i, distance).wait_send()

    for i in range(2):

        @pl.when(even)
        def _():
            fw_copy(i, 0, 1).wait_send()

        @pl.when(even & (shard >= 2))
        def _():
            fw_copy(i, 2, 3).wait_send()

        @pl.when(jnp.logical_not(even) & (shard >= 2))
        def _():
            fw_copy(i, 2, 1).wait_send()

        @pl.when(jnp.logical_not(even) & (shard >= 4))
        def _():
            fw_copy(i, 4, 3).wait_send()

        for distance in range(1, REACH + 1):

            @pl.when(shard >= distance)
            def _():
                grad_copy(i, distance).wait_send()

    for c in range(CHUNKS):
        for d in range(n_t):

            @pl.when(t < d)
            def _():
                right_copy(c, d).wait_send()

            @pl.when(t > d)
            def _():
                left_copy(c, d).wait_send()


def shards(sizes, queries, keys, values, doc_lengths, w_out, d_out):
    n_t = sizes[2]
    rows, q_width = queries.shape
    kv_width = keys.shape[1]
    groups = kv_width // HEAD
    heads = q_width // HEAD
    per = heads // groups
    chunk = rows // CHUNKS
    ext = (REACH + 1) * rows
    window = REACH * rows + chunk
    d_model = w_out.shape[1]
    width = d_model // n_t
    bf, f32 = jnp.bfloat16, jnp.float32
    all_rows = per * rows
    n_w = 4
    anywhere = pl.BlockSpec(memory_space=pl.ANY)
    vmem = pl.BlockSpec(memory_space=pltpu.VMEM)
    dma = pltpu.SemaphoreType.DMA
    return pl.pallas_call(
        functools.partial(kernel, sizes),
        out_shape=(
            jax.ShapeDtypeStruct((rows, width), bf),
            jax.ShapeDtypeStruct((rows, q_width), bf),
            jax.ShapeDtypeStruct((rows, kv_width), bf),
            jax.ShapeDtypeStruct((rows, kv_width), bf),
        ),
        in_specs=[
            anywhere, anywhere, anywhere, pl.BlockSpec(memory_space=pltpu.SMEM), anywhere, anywhere,
        ],
        out_specs=(vmem,) * 4,
        scratch_shapes=[
            pltpu.VMEM((rows, q_width), bf),
            pltpu.VMEM((rows, d_model), bf),
            pltpu.VMEM(w_out.shape, bf),
            pltpu.VMEM((ext, kv_width), bf),
            pltpu.VMEM((ext, kv_width), bf),
            pltpu.VMEM((groups, all_rows, HEAD), bf),
            pltpu.VMEM((groups, all_rows, HEAD), bf),
            pltpu.VMEM((CHUNKS, chunk, q_width), bf),
            pltpu.VMEM((CHUNKS, chunk, window), f32),
            pltpu.VMEM((per * chunk, window), f32),
            pltpu.VMEM((groups, all_rows, ext), bf),
            pltpu.VMEM((groups, all_rows, 1), f32),
            pltpu.VMEM((all_rows, rows), f32),
            pltpu.VMEM((all_rows, rows), bf),
            pltpu.VMEM((groups, all_rows, HEAD), f32),
            pltpu.VMEM((REACH, rows, kv_width), bf),
            pltpu.VMEM((REACH, rows, kv_width), bf),
            pltpu.VMEM((REACH, rows, kv_width), bf),
            pltpu.VMEM((REACH, rows, kv_width), bf),
            pltpu.VMEM((2, rows, kv_width), f32),
            pltpu.VMEM((CHUNKS, n_t, chunk, width), bf),
            pltpu.VMEM((CHUNKS, n_t, chunk, width), bf),
            pltpu.VMEM((CHUNKS, n_t, chunk, width), bf),
            dma((4,)),
            dma((n_w,)),
            dma((4,)),
            dma((4,)),
            dma((4,)),
            dma((4,)),
            dma((2, REACH)),
            dma((2, REACH)),
            dma((CHUNKS, n_t)),
            dma((CHUNKS, n_t)),
            dma((CHUNKS, n_t)),
            dma((CHUNKS, n_t)),
        ],
        compiler_params=pltpu.CompilerParams(
            collective_id=0, has_side_effects=True, vmem_limit_bytes=60 * 1024 * 1024
        ),
        name="layer",
    )(queries, keys, values, doc_lengths, w_out, d_out)


def solution(mesh):
    sizes = tuple(mesh.shape[a] for a in ("seq", "server", "tensor"))
    tokens = P(("seq", "server"), "tensor")
    return jax.shard_map(
        functools.partial(shards, sizes),
        mesh=mesh,
        in_specs=(tokens, tokens, tokens, P(), P("tensor", None), P(("seq", "server"), None)),
        out_specs=(tokens,) * 4,
        check_vma=False,
    )
```

time: 144 us -> 92.2 us (0.64); the launches traced: 142 us -> 91.9 us
  Pallas kernels: 0 us -> 84.4 us
  matrix products: 37.7 us -> 0 us
  starting transfers between devices: 31.1 us -> 0 us
  local copies, waits for them, and re-layouts: 33.6 us -> 6.87 us
  between operations: 14.6 us -> 0.64 us
  other arithmetic: 13.6 us -> 0 us
  waiting for transfers between devices: 10.9 us -> 0 us
    pallas_call x0 -> x1, Pallas kernels: none -> 84.4 us  [shards(): pl.pallas_call(functools.partial(kernel, sizes), out_shape=(jax.ShapeDtyp...]
    ppermute x16 -> x0, starting transfers between devices: 31.1 us -> none  [shifted(): return lax.ppermute(block, axis, route)]
    dot_general x12 -> x0, matrix products: 27.7 us -> none  [the longest x1 7.07 us: shards(): jnp.dot(attn, w_out, preferred_element_type=jnp.float32)]
    slice x17 -> x0, local copies, waits for them, and re-layouts: 11.3 us -> none  [the longest x3 3.33 us: shards(): ext_values[row_start:row_start + window_span]]
    ppermute x16 -> x0, waiting for transfers between devices: 10.9 us -> none  [shifted(): return lax.ppermute(block, axis, route)]
    convert_element_type x4 -> x0, other arithmetic: 10.1 us -> none  [the longest x2 7.51 us: block_window(): lower_shares = shares.astype(jnp.bfloat16)]
    sub x2 -> x0, matrix products: 9.97 us -> none  [block_window(): weights = jnp.exp(masked - row_top)]
    convert_element_type x8 -> x0, local copies, waits for them, and re-layouts: 6.96 us -> none  [the longest x4 3.95 us: shards(): partial_key.astype(jnp.bfloat16)]
  transfers between devices with their start and end apart: 17 -> 0, of which waited for: 4 -> 0; matrix products, arithmetic and copies ran while one was open for 33% -> 0% of each run, Pallas kernels for 0% -> 0%
where the time goes in v1:
time: 92.2 us; the launch traced here: 91.9 us
  Pallas kernels  84.4 us (92%)
  local copies, waits for them, and re-layouts  6.87 us (7%)
    pallas_call x1, Pallas kernels, shards(): pl.pallas_call(functools.partial(kernel, sizes), out_shape=(jax.ShapeDtyp...  84.4 us
    unnamed x4, local copies, waits for them, and re-layouts  6.87 us

profile of v1, /device:TPU:2, one launch (start us, length us, event | category | flops | bytes accessed | tf_op | source)
XLA Modules:
  0.0 91.9 jit_solution(12612864464847492757)
XLA Ops:
  0.6 84.4 %layer.1 = (bf16[256,1024]{1,0:T(8,128)(2,1)}, bf16[256,1024]{1,0:T(8,128)(2,1)}, bf16[256,256]{1,0:T(8,128)(2,1)}, bf16[256,256]{1,0:T(8,128)(2,1)}) custom-call(bf16[256,1024]{1,0:T(8,128)(2,1)} %q_hbm.1, bf16[256,256]{1,0:T(8,128)(2,1)} %k_hbm.1, bf16[256,256]{1,0:T(8,128)(2,1)} %v_hbm.1, s32[4]{0:T(128)} %doc.1, bf16[1024,4096]{1,0:T(8,128)(2,1)} %w_hbm.1, ...), custom_call_target="tpu_custom_call" | custom-call | tf_op jit(solution)/shard_map/layer/pallas_call | solution.py:449
  85.0 1.9 %copy.14 = bf16[256,1024]{1,0:T(8,128)(2,1)} copy(bf16[256,1024]{1,0:T(8,128)(2,1)} %get-tuple-element.8) | data formatting | bytes 1048576
  86.9 1.9 %copy.15 = bf16[256,1024]{1,0:T(8,128)(2,1)} copy(bf16[256,1024]{1,0:T(8,128)(2,1)} %get-tuple-element.9) | data formatting | bytes 1048576
  88.8 1.6 %copy.16 = bf16[256,256]{1,0:T(8,128)(2,1)} copy(bf16[256,256]{1,0:T(8,128)(2,1)} %get-tuple-element.10) | data formatting | bytes 262144
  90.4 1.6 %copy.17 = bf16[256,256]{1,0:T(8,128)(2,1)} copy(bf16[256,256]{1,0:T(8,128)(2,1)} %get-tuple-element.11) | data formatting | bytes 262144

commit v2 on v1

--- a/solution.py
+++ b/solution.py
@@ -26,8 +26,8 @@
     q_hbm, k_hbm, v_hbm, doc, w_hbm, do_hbm,
     out_ref, gq_ref, gk_ref, gv_ref,
     q_in, do_in, w, kx, vx, qs, dos, attn, bias, s_ref, p_ref, delta,
-    dp_ref, ds_ref, dq_acc, gsk, gsv, grk, grv, gown, part, rr, rl,
-    loc_sem, w_sem, kv_send, kv_recv, fw_send, fw_recv, g_send, g_recv,
+    dp_ref, ds_ref, dq_acc, gsk, gsv, gpk, gpv, grk, grv, gown, part, rr, rl,
+    loc_sem, w_sem, kv_send, kv_recv, fw_send, fw_recv, p_send, p_recv, g_send, g_recv,
     r_send, r_recv, l_send, l_recv,
 ):
     n_seq, n_server, n_t = sizes
@@ -71,7 +71,10 @@
 
     barrier = pltpu.get_barrier_semaphore()
     count = jnp.int32(0)
-    for step in range(1, REACH + 1):
+    partner = shard + 1 - 2 * lax.rem(shard, 2)
+    pl.semaphore_signal(barrier, inc=1, device_id=at_shard(partner), device_id_type=MESH)
+    count = count + 1
+    for step in (2, 4):
         for sign in (1, -1):
             other = shard + sign * step
             ok = (other >= 0) & (other < n_shards)
@@ -108,7 +111,6 @@
         )
 
     even = lax.rem(shard, 2) == 0
-    partner = shard + 1 - 2 * lax.rem(shard, 2)
 
     def fw_copy(i, from_distance, to_distance):
         ref = (kx, vx)[i]
@@ -122,11 +124,11 @@
             device_id_type=MESH,
         )
 
-    for distance in (4, 2):
-
-        @pl.when(shard + distance < n_shards)
-        def _():
-            for i in range(2):
+    for i in range(2):
+        for distance in (4, 2):
+
+            @pl.when(shard + distance < n_shards)
+            def _():
                 kv_copy(i, distance).start()
 
     for c in loads[:2]:
@@ -178,39 +180,33 @@
                 if tail > 0:
                     p_ref[g, place, pl.ds(ext - tail, tail)] = jnp.zeros((crows, tail), jnp.bfloat16)
 
-    @pl.when(shard >= 2)
-    def _():
-        for i in range(2):
+    def arrive(i):
+        @pl.when(shard >= 4)
+        def _():
+            kv_copy(i, 4).wait_recv()
+
+            @pl.when(jnp.logical_not(even))
+            def _():
+                fw_copy(i, 4, 3).start()
+
+        @pl.when(shard >= 2)
+        def _():
             kv_copy(i, 2).wait_recv()
 
-        @pl.when(even)
-        def _():
-            for i in range(2):
+            @pl.when(even)
+            def _():
                 fw_copy(i, 2, 3).start()
 
-        @pl.when(jnp.logical_not(even))
-        def _():
-            for i in range(2):
+            @pl.when(jnp.logical_not(even))
+            def _():
                 fw_copy(i, 2, 1).start()
 
-    @pl.when(shard >= 4)
-    def _():
-        for i in range(2):
-            kv_copy(i, 4).wait_recv()
-
-        @pl.when(jnp.logical_not(even))
-        def _():
-            for i in range(2):
-                fw_copy(i, 4, 3).start()
-
-    @pl.when(shard >= 1)
-    def _():
-        for i in range(2):
+        @pl.when(shard >= 1)
+        def _():
             fw_copy(i, 0, 1).wait_recv()
 
-    @pl.when(shard >= 3)
-    def _():
-        for i in range(2):
+        @pl.when(shard >= 3)
+        def _():
             fw_copy(i, 2, 3).wait_recv()
 
     order = []
@@ -265,6 +261,7 @@
     factor = scale * math.log2(math.e)
     blocks = crows // ROW_BLOCK
     per_head = chunk // ROW_BLOCK
+    arrive(0)
     for c in range(CHUNKS):
         place = pl.ds(c * crows, crows)
         win = pl.ds(c * chunk, window)
@@ -272,7 +269,7 @@
             gc = pl.ds(g * HEAD, HEAD)
             s_ref[...] = dot(qs[g, place], kx[win, gc], NT)
 
-            @pl.loop(0, blocks, unroll=2)
+            @pl.loop(0, blocks, unroll=4)
             def _(b):
                 row = pl.multiple_of(b * ROW_BLOCK, ROW_BLOCK)
                 brow = pl.multiple_of(lax.rem(b, per_head) * ROW_BLOCK, ROW_BLOCK)
@@ -282,6 +279,10 @@
                 inv = 1.0 / jnp.sum(e, axis=1, keepdims=True)
                 p_ref[g, pl.ds(c * crows + row, ROW_BLOCK), win] = (e * inv).astype(jnp.bfloat16)
 
+        if c == 0:
+            arrive(1)
+        for g in range(groups):
+            gc = pl.ds(g * HEAD, HEAD)
             o = dot(p_ref[g, place, win], vx[win, gc]).astype(jnp.bfloat16)
             delta[g, place] = jnp.sum(
                 o.astype(jnp.float32) * dos[g, place].astype(jnp.float32), axis=1, keepdims=True
@@ -302,51 +303,104 @@
                 def _():
                     left_copy(c, d).start()
 
+    def pair_copy(i, distance):
+        src, dst = ((gsk, gpk), (gsv, gpv))[i]
+        e = distance // 2
+        return pltpu.make_async_remote_copy(
+            src_ref=src.at[distance - 1],
+            dst_ref=dst.at[e],
+            send_sem=p_send.at[i, e],
+            recv_sem=p_recv.at[i, e],
+            device_id=at_shard(partner),
+            device_id_type=MESH,
+        )
+
     def grad_copy(i, distance):
         src, dst = ((gsk, grk), (gsv, grv))[i]
+        e = distance // 2 - 1
         return pltpu.make_async_remote_copy(
             src_ref=src.at[distance - 1],
-            dst_ref=dst.at[distance - 1],
-            send_sem=g_send.at[i, distance - 1],
-            recv_sem=g_recv.at[i, distance - 1],
+            dst_ref=dst.at[e],
+            send_sem=g_send.at[i, e],
+            recv_sem=g_recv.at[i, e],
             device_id=at_shard(shard - distance),
             device_id_type=MESH,
         )
 
-    for kb in range(REACH + 1):
-        distance = REACH - kb
-        keys = pl.ds(kb * rows, rows)
+    def merge(i, distance, came):
+        own, got = ((gsk, gpk), (gsv, gpv))[i]
+        pair_copy(i, came).wait_recv()
+        own[distance - 1] = (
+            own[distance - 1].astype(jnp.float32) + got[came // 2].astype(jnp.float32)
+        ).astype(jnp.bfloat16)
+
+    for distance in (3, 1, 4, 2, 0):
+        keys = slot(distance)
         for g in range(groups):
             gc = pl.ds(g * HEAD, HEAD)
             dp_ref[...] = dot(dos[g], vx[keys, gc], NT)
-            ds_ref[...] = (p_ref[g, :, keys].astype(jnp.float32) * (dp_ref[...] - delta[g])).astype(
-                jnp.bfloat16
-            )
+            kcols = pl.ds((REACH - distance) * rows, rows)
+            ds_ref[...] = (
+                p_ref[g, :, kcols].astype(jnp.float32) * (dp_ref[...] - delta[g])
+            ).astype(jnp.bfloat16)
             dq = dot(ds_ref[...], kx[keys, gc])
-            if kb == 0:
+            if distance == 3:
                 dq_acc[g] = dq
             else:
                 dq_acc[g] += dq
             dk = dot(ds_ref[...], qs[g], TN) * scale
-            dv = dot(p_ref[g, :, keys], dos[g], TN)
+            dv = dot(p_ref[g, :, kcols], dos[g], TN)
             if distance > 0:
                 gsk[distance - 1, :, gc] = dk.astype(jnp.bfloat16)
                 gsv[distance - 1, :, gc] = dv.astype(jnp.bfloat16)
             else:
                 gown[0, :, gc] = dk
                 gown[1, :, gc] = dv
-        if distance > 0:
+        if distance in (1, 3):
 
             @pl.when(shard >= distance)
             def _():
                 for i in range(2):
-                    grad_copy(i, distance).start()
-
-        if kb == 2:
+                    pair_copy(i, distance).start()
+
+        if distance == 4:
+
+            @pl.when(shard >= 4)
+            def _():
+                for i in range(2):
+
+                    @pl.when(jnp.logical_not(even))
+                    def _():
+                        merge(i, 4, 3)
+
+                    grad_copy(i, 4).start()
+
+        if distance == 2:
+
+            @pl.when(shard >= 2)
+            def _():
+                for i in range(2):
+
+                    @pl.when(jnp.logical_not(even))
+                    def _():
+                        merge(i, 2, 1)
+
+                    @pl.when(even)
+                    def _():
+                        merge(i, 2, 3)
+
+                    grad_copy(i, 2).start()
+
             relay(0, n_t - 1)
-        if kb == 4:
-            for d in range(n_t - 2, 0, -1):
-                relay(0, d)
+
+    @pl.when(even)
+    def _():
+        for i, ref in enumerate((gpk, gpv)):
+            pair_copy(i, 1).wait_recv()
+            gown[i] += ref[0].astype(jnp.float32)
+
+    for d in range(n_t - 2, 0, -1):
+        relay(0, d)
 
     for g in range(groups):
         for c in range(CHUNKS):
@@ -359,13 +413,13 @@
         for d in range(n_t - 1, 0, -1):
             relay(c, d)
 
-    for distance in range(REACH, 0, -1):
+    for distance in (4, 2):
 
         @pl.when(shard + distance < n_shards)
         def _():
             for i, ref in enumerate((grk, grv)):
                 grad_copy(i, distance).wait_recv()
-                gown[i] += ref[distance - 1].astype(jnp.float32)
+                gown[i] += ref[distance // 2 - 1].astype(jnp.float32)
 
     gk_ref[...] = gown[0].astype(jnp.bfloat16)
     gv_ref[...] = gown[1].astype(jnp.bfloat16)
@@ -414,7 +468,10 @@
 
             @pl.when(shard >= distance)
             def _():
-                grad_copy(i, distance).wait_send()
+                if distance % 2:
+                    pair_copy(i, distance).wait_send()
+                else:
+                    grad_copy(i, distance).wait_send()
 
     for c in range(CHUNKS):
         for d in range(n_t):
@@ -426,6 +483,19 @@
             @pl.when(t > d)
             def _():
                 left_copy(c, d).wait_send()
+
+
+def hand_over(*refs):
+    sources, targets, held, in_sem, out_sem = refs[:4], refs[4:8], refs[8:12], refs[12], refs[13]
+    ins = [pltpu.make_async_copy(sources[i], held[i], in_sem.at[i]) for i in range(4)]
+    outs = [pltpu.make_async_copy(held[i], targets[i], out_sem.at[i]) for i in range(4)]
+    for c in ins:
+        c.start()
+    for i in range(4):
+        ins[i].wait()
+        outs[i].start()
+    for c in outs:
+        c.wait()
 
 
 def shards(sizes, queries, keys, values, doc_lengths, w_out, d_out):
@@ -446,7 +516,7 @@
     anywhere = pl.BlockSpec(memory_space=pl.ANY)
     vmem = pl.BlockSpec(memory_space=pltpu.VMEM)
     dma = pltpu.SemaphoreType.DMA
-    return pl.pallas_call(
+    results = pl.pallas_call(
         functools.partial(kernel, sizes),
         out_shape=(
             jax.ShapeDtypeStruct((rows, width), bf),
@@ -476,8 +546,10 @@
             pltpu.VMEM((groups, all_rows, HEAD), f32),
             pltpu.VMEM((REACH, rows, kv_width), bf),
             pltpu.VMEM((REACH, rows, kv_width), bf),
-            pltpu.VMEM((REACH, rows, kv_width), bf),
-            pltpu.VMEM((REACH, rows, kv_width), bf),
+            pltpu.VMEM((2, rows, kv_width), bf),
+            pltpu.VMEM((2, rows, kv_width), bf),
+            pltpu.VMEM((2, rows, kv_width), bf),
+            pltpu.VMEM((2, rows, kv_width), bf),
             pltpu.VMEM((2, rows, kv_width), f32),
             pltpu.VMEM((CHUNKS, n_t, chunk, width), bf),
             pltpu.VMEM((CHUNKS, n_t, chunk, width), bf),
@@ -488,8 +560,10 @@
             dma((4,)),
             dma((4,)),
             dma((4,)),
-            dma((2, REACH)),
-            dma((2, REACH)),
+            dma((2, 2)),
+            dma((2, 2)),
+            dma((2, 2)),
+            dma((2, 2)),
             dma((CHUNKS, n_t)),
             dma((CHUNKS, n_t)),
             dma((CHUNKS, n_t)),
@@ -500,6 +574,14 @@
         ),
         name="layer",
     )(queries, keys, values, doc_lengths, w_out, d_out)
+    return pl.pallas_call(
+        hand_over,
+        out_shape=tuple(jax.ShapeDtypeStruct(x.shape, x.dtype) for x in results),
+        in_specs=[anywhere] * 4,
+        out_specs=(anywhere,) * 4,
+        scratch_shapes=[pltpu.VMEM(x.shape, x.dtype) for x in results] + [dma((4,)), dma((4,))],
+        name="hand_over",
+    )(*results)
 
 
 def solution(mesh):

time: 92.2 us -> 78.3 us (0.85)
  Pallas kernels: 84.4 us -> 77.3 us
  local copies, waits for them, and re-layouts: 6.87 us -> 0 us
    pallas_call x1, Pallas kernels: 84.4 us -> 75.1 us  [shards(): pl.pallas_call(functools.partial(kernel, sizes), out_shape=(jax.ShapeDtyp...]
    unnamed x4 -> x0, local copies, waits for them, and re-layouts: 6.87 us -> none
    pallas_call x0 -> x1, Pallas kernels: none -> 2.15 us  [shards(): pl.pallas_call(hand_over, out_shape=tuple((jax.ShapeDtypeStruct(x.shape,...]
where the time goes in v2:
time: 78.3 us; the launch traced here: 78.1 us
  Pallas kernels  77.3 us (99%)
  between operations  0.82 us (1%)
    pallas_call x1, Pallas kernels, shards(): pl.pallas_call(functools.partial(kernel, sizes), out_shape=(jax.ShapeDtyp...  75.1 us
    pallas_call x1, Pallas kernels, shards(): pl.pallas_call(hand_over, out_shape=tuple((jax.ShapeDtypeStruct(x.shape,...  2.15 us

profile of v2, /device:TPU:2, one launch (start us, length us, event | category | flops | bytes accessed | tf_op | source)
XLA Modules:
  0.0 78.1 jit_solution(8269438286004655616)
XLA Ops:
  0.6 75.1 %layer.1 = (bf16[256,1024]{1,0:T(8,128)(2,1)}, bf16[256,1024]{1,0:T(8,128)(2,1)}, bf16[256,256]{1,0:T(8,128)(2,1)}, bf16[256,256]{1,0:T(8,128)(2,1)}) custom-call(bf16[256,1024]{1,0:T(8,128)(2,1)} %q_hbm.1, bf16[256,256]{1,0:T(8,128)(2,1)} %k_hbm.1, bf16[256,256]{1,0:T(8,128)(2,1)} %v_hbm.1, s32[4]{0:T(128)} %doc.1, bf16[1024,4096]{1,0:T(8,128)(2,1)} %w_hbm.1, ...), custom_call_target="tpu_custom_call" | custom-call | tf_op jit(solution)/shard_map/layer/pallas_call | solution.py:519
  75.8 2.2 %hand_over.1 = (bf16[256,1024]{1,0:T(8,128)(2,1)}, bf16[256,1024]{1,0:T(8,128)(2,1)}, bf16[256,256]{1,0:T(8,128)(2,1)}, bf16[256,256]{1,0:T(8,128)(2,1)}) custom-call(bf16[256,1024]{1,0:T(8,128)(2,1)} %get-tuple-element.8.refs_0_, bf16[256,1024]{1,0:T(8,128)(2,1)} %get-tuple-element.9.refs_1_, bf16[256,256]{1,0:T(8,128)(2,1)} %get-tuple-element.10.refs_2_, ...), custom_call_target="tpu_custom_call" | custom-call | tf_op jit(solution)/shard_map/hand_over/pallas_call | solution.py:577

commit v3 on v2

--- a/solution.py
+++ b/solution.py
@@ -238,25 +238,29 @@
             device_id_type=MESH,
         )
 
-    def relay(c, d):
-        e = n_t - 1 - d
-        if d > 0:
-
-            @pl.when((t > 0) & (t < d))
-            def _():
-                right_copy(c, d).wait_recv()
-                part[c, d] = (part[c, d].astype(jnp.float32) + rr[c, d].astype(jnp.float32)).astype(
-                    jnp.bfloat16
-                )
-                right_copy(c, d).start()
-
-            @pl.when((t < n_t - 1) & (t > e))
-            def _():
-                left_copy(c, e).wait_recv()
-                part[c, e] = (part[c, e].astype(jnp.float32) + rl[c, e].astype(jnp.float32)).astype(
-                    jnp.bfloat16
-                )
-                left_copy(c, e).start()
+    def pass_on(copy, came, c, d):
+        copy(c, d).wait_recv()
+        part[c, d] = (part[c, d].astype(jnp.float32) + came[c, d].astype(jnp.float32)).astype(
+            jnp.bfloat16
+        )
+        copy(c, d).start()
+
+    def relay(c, step):
+        for here in range(1, n_t - 1):
+            right = [(k + here, 0, n_t - 1 - k) for k in range(n_t - 1 - here)]
+            left = [(k + n_t - 1 - here, 1, k) for k in range(here)]
+            due = [x for x in sorted(right + left) if x[0] == step]
+            if 2 * here >= n_t:
+                due = due[::-1]
+            if due:
+
+                @pl.when(t == here)
+                def _():
+                    for _, way, d in due:
+                        if way == 0:
+                            pass_on(right_copy, rr, c, d)
+                        else:
+                            pass_on(left_copy, rl, c, d)
 
     factor = scale * math.log2(math.e)
     blocks = crows // ROW_BLOCK
@@ -289,19 +293,26 @@
             )
             for r in range(per):
                 attn[c, :, pl.ds((g * per + r) * HEAD, HEAD)] = o[r * chunk : (r + 1) * chunk]
+        done, right_next, left_next = [], n_t - 1, 0
         for d in order:
             part[c, d] = dot(attn[c], w[:, cols(d)]).astype(jnp.bfloat16)
-            if d > 0:
+            done.append(d)
+            while right_next > 0 and right_next in done:
+                d_right = right_next
 
                 @pl.when(t == 0)
                 def _():
-                    right_copy(c, d).start()
-
-            if d < n_t - 1:
+                    right_copy(c, d_right).start()
+
+                right_next -= 1
+            while left_next < n_t - 1 and left_next in done:
+                d_left = left_next
 
                 @pl.when(t == n_t - 1)
                 def _():
-                    left_copy(c, d).start()
+                    left_copy(c, d_left).start()
+
+                left_next += 1
 
     def pair_copy(i, distance):
         src, dst = ((gsk, gpk), (gsv, gpv))[i]
@@ -334,7 +345,10 @@
             own[distance - 1].astype(jnp.float32) + got[came // 2].astype(jnp.float32)
         ).astype(jnp.bfloat16)
 
+    relay(0, 1)
     for distance in (3, 1, 4, 2, 0):
+        if distance == 2:
+            relay(0, 2)
         keys = slot(distance)
         for g in range(groups):
             gc = pl.ds(g * HEAD, HEAD)
@@ -391,16 +405,14 @@
 
                     grad_copy(i, 2).start()
 
-            relay(0, n_t - 1)
-
     @pl.when(even)
     def _():
         for i, ref in enumerate((gpk, gpv)):
             pair_copy(i, 1).wait_recv()
             gown[i] += ref[0].astype(jnp.float32)
 
-    for d in range(n_t - 2, 0, -1):
-        relay(0, d)
+    for step in range(3, n_t - 1):
+        relay(0, step)
 
     for g in range(groups):
         for c in range(CHUNKS):
@@ -410,8 +422,8 @@
                 ).astype(jnp.bfloat16)
 
     for c in range(1, CHUNKS):
-        for d in range(n_t - 1, 0, -1):
-            relay(c, d)
+        for step in range(1, n_t - 1):
+            relay(c, step)
 
     for distance in (4, 2):
 

time: 78.3 us -> 63.1 us (0.81)
  Pallas kernels: 77.3 us -> 62.1 us
    pallas_call x1, Pallas kernels: 75.1 us -> 60 us  [shards(): pl.pallas_call(functools.partial(kernel, sizes), out_shape=(jax.ShapeDtyp...]
where the time goes in v3:
time: 63.1 us; the launch traced here: 62.9 us
  Pallas kernels  62.1 us (98%)
  between operations  0.8 us (1%)
    pallas_call x1, Pallas kernels, shards(): pl.pallas_call(functools.partial(kernel, sizes), out_shape=(jax.ShapeDtyp...  60 us
    pallas_call x1, Pallas kernels, shards(): pl.pallas_call(hand_over, out_shape=tuple((jax.ShapeDtypeStruct(x.shape,...  2.15 us

profile of v3, /device:TPU:2, one launch (start us, length us, event | category | flops | bytes accessed | tf_op | source)
XLA Modules:
  0.0 62.9 jit_solution(2774798695267393730)
XLA Ops:
  0.6 60.0 %layer.1 = (bf16[256,1024]{1,0:T(8,128)(2,1)}, bf16[256,1024]{1,0:T(8,128)(2,1)}, bf16[256,256]{1,0:T(8,128)(2,1)}, bf16[256,256]{1,0:T(8,128)(2,1)}) custom-call(bf16[256,1024]{1,0:T(8,128)(2,1)} %q_hbm.1, bf16[256,256]{1,0:T(8,128)(2,1)} %k_hbm.1, bf16[256,256]{1,0:T(8,128)(2,1)} %v_hbm.1, s32[4]{0:T(128)} %doc.1, bf16[1024,4096]{1,0:T(8,128)(2,1)} %w_hbm.1, ...), custom_call_target="tpu_custom_call" | custom-call | tf_op jit(solution)/shard_map/layer/pallas_call | solution.py:531
  60.6 2.2 %hand_over.1 = (bf16[256,1024]{1,0:T(8,128)(2,1)}, bf16[256,1024]{1,0:T(8,128)(2,1)}, bf16[256,256]{1,0:T(8,128)(2,1)}, bf16[256,256]{1,0:T(8,128)(2,1)}) custom-call(bf16[256,1024]{1,0:T(8,128)(2,1)} %get-tuple-element.8.refs_0_, bf16[256,1024]{1,0:T(8,128)(2,1)} %get-tuple-element.9.refs_1_, bf16[256,256]{1,0:T(8,128)(2,1)} %get-tuple-element.10.refs_2_, ...), custom_call_target="tpu_custom_call" | custom-call | tf_op jit(solution)/shard_map/hand_over/pallas_call | solution.py:589

commit v4 on v3

--- a/solution.py
+++ b/solution.py
@@ -160,6 +160,38 @@
                 dos[g, place] = d[c * chunk : (c + 1) * chunk, a * HEAD : (a + 1) * HEAD]
                 qs[g, place] = q_in[pl.ds(c * chunk, chunk), pl.ds(h * HEAD, HEAD)]
 
+    def arrive(i):
+        @pl.when(shard >= 4)
+        def _():
+            kv_copy(i, 4).wait_recv()
+
+            @pl.when(jnp.logical_not(even))
+            def _():
+                fw_copy(i, 4, 3).start()
+
+        @pl.when(shard >= 2)
+        def _():
+            kv_copy(i, 2).wait_recv()
+
+            @pl.when(even)
+            def _():
+                fw_copy(i, 2, 3).start()
+
+            @pl.when(jnp.logical_not(even))
+            def _():
+                fw_copy(i, 2, 1).start()
+
+    def arrived(i):
+        @pl.when(shard >= 1)
+        def _():
+            fw_copy(i, 0, 1).wait_recv()
+
+        @pl.when(shard >= 3)
+        def _():
+            fw_copy(i, 2, 3).wait_recv()
+
+    arrive(0)
+
     for c in range(CHUNKS):
         first = shard * rows + c * chunk
         q_pos = first + lax.broadcasted_iota(jnp.int32, (chunk, 1), 0)
@@ -180,35 +212,6 @@
                 if tail > 0:
                     p_ref[g, place, pl.ds(ext - tail, tail)] = jnp.zeros((crows, tail), jnp.bfloat16)
 
-    def arrive(i):
-        @pl.when(shard >= 4)
-        def _():
-            kv_copy(i, 4).wait_recv()
-
-            @pl.when(jnp.logical_not(even))
-            def _():
-                fw_copy(i, 4, 3).start()
-
-        @pl.when(shard >= 2)
-        def _():
-            kv_copy(i, 2).wait_recv()
-
-            @pl.when(even)
-            def _():
-                fw_copy(i, 2, 3).start()
-
-            @pl.when(jnp.logical_not(even))
-            def _():
-                fw_copy(i, 2, 1).start()
-
-        @pl.when(shard >= 1)
-        def _():
-            fw_copy(i, 0, 1).wait_recv()
-
-        @pl.when(shard >= 3)
-        def _():
-            fw_copy(i, 2, 3).wait_recv()
-
     order = []
     for a in range((n_t + 1) // 2):
         order.append(n_t - 1 - a)
@@ -265,7 +268,7 @@
     factor = scale * math.log2(math.e)
     blocks = crows // ROW_BLOCK
     per_head = chunk // ROW_BLOCK
-    arrive(0)
+    arrived(0)
     for c in range(CHUNKS):
         place = pl.ds(c * crows, crows)
         win = pl.ds(c * chunk, window)
@@ -283,8 +286,11 @@
                 inv = 1.0 / jnp.sum(e, axis=1, keepdims=True)
                 p_ref[g, pl.ds(c * crows + row, ROW_BLOCK), win] = (e * inv).astype(jnp.bfloat16)
 
+            if c == 0 and g == 0:
+                arrive(1)
+
         if c == 0:
-            arrive(1)
+            arrived(1)
         for g in range(groups):
             gc = pl.ds(g * HEAD, HEAD)
             o = dot(p_ref[g, place, win], vx[win, gc]).astype(jnp.bfloat16)

time: 63.1 us -> 61.6 us (0.976)
  Pallas kernels: 62.1 us -> 60.6 us
    pallas_call x1, Pallas kernels: 60 us -> 58.5 us  [shards(): pl.pallas_call(functools.partial(kernel, sizes), out_shape=(jax.ShapeDtyp...]
where the time goes in v4:
time: 61.6 us; the launch traced here: 61.4 us
  Pallas kernels  60.6 us (98%)
  between operations  0.8 us (1%)
    pallas_call x1, Pallas kernels, shards(): pl.pallas_call(functools.partial(kernel, sizes), out_shape=(jax.ShapeDtyp...  58.5 us
    pallas_call x1, Pallas kernels, shards(): pl.pallas_call(hand_over, out_shape=tuple((jax.ShapeDtypeStruct(x.shape,...  2.15 us

profile of v4, /device:TPU:2, one launch (start us, length us, event | category | flops | bytes accessed | tf_op | source)
XLA Modules:
  0.0 61.4 jit_solution(12974708768306173290)
XLA Ops:
  0.6 58.5 %layer.1 = (bf16[256,1024]{1,0:T(8,128)(2,1)}, bf16[256,1024]{1,0:T(8,128)(2,1)}, bf16[256,256]{1,0:T(8,128)(2,1)}, bf16[256,256]{1,0:T(8,128)(2,1)}) custom-call(bf16[256,1024]{1,0:T(8,128)(2,1)} %q_hbm.1, bf16[256,256]{1,0:T(8,128)(2,1)} %k_hbm.1, bf16[256,256]{1,0:T(8,128)(2,1)} %v_hbm.1, s32[4]{0:T(128)} %doc.1, bf16[1024,4096]{1,0:T(8,128)(2,1)} %w_hbm.1, ...), custom_call_target="tpu_custom_call" | custom-call | tf_op jit(solution)/shard_map/layer/pallas_call | solution.py:537
  59.1 2.2 %hand_over.1 = (bf16[256,1024]{1,0:T(8,128)(2,1)}, bf16[256,1024]{1,0:T(8,128)(2,1)}, bf16[256,256]{1,0:T(8,128)(2,1)}, bf16[256,256]{1,0:T(8,128)(2,1)}) custom-call(bf16[256,1024]{1,0:T(8,128)(2,1)} %get-tuple-element.8.refs_0_, bf16[256,1024]{1,0:T(8,128)(2,1)} %get-tuple-element.9.refs_1_, bf16[256,256]{1,0:T(8,128)(2,1)} %get-tuple-element.10.refs_2_, ...), custom_call_target="tpu_custom_call" | custom-call | tf_op jit(solution)/shard_map/hand_over/pallas_call | solution.py:595
